TPU v7x, 32 devices: a whole 2x2x4 slice. The times are simulated.
32 devices in a mesh: gx: 4 (over x, core), yz: 8 (over z, y).
Axes of the slice: x: 2, y: 2, z: 4, core: 2. Of those that a mesh axis runs over, the one named last changes fastest.
Arguments:
- stream: bfloat16 [128, 9216], P('yz', 'gx'), may hold values from -1700 to 1700
- ln_gain: bfloat16 [9216], P('gx'), may hold values from 0.099609375 to 1.8984375
- q_weight: bfloat16 [9216, 12288], P('gx', 'yz'), may hold values from -0.0625 to 0.0625
- kv_weight: bfloat16 [9216, 512], P('gx', 'yz'), may hold values from -0.0625 to 0.0625
- out_weight: bfloat16 [12288, 9216], P('yz', 'gx'), may hold values from -0.0546875 to 0.0546875
- gate_weight: bfloat16 [9216, 36864], P('gx', 'yz'), may hold values from -0.0625 to 0.0625
- up_weight: bfloat16 [9216, 36864], P('gx', 'yz'), may hold values from -0.0625 to 0.0625
- down_weight: bfloat16 [36864, 9216], P('yz', 'gx'), may hold values from -0.03125 to 0.03125
- cache: bfloat16 [128, 1536, 512], P(('gx', 'yz')), may hold values from -620 to 620
- lengths: int32 [128], P(('gx', 'yz')), may hold values from 1 to 1536, as said below
Outputs:
- update: bfloat16 [128, 9216], P('yz', 'gx')
Inputs may be any that keep to these rules, and one draw needn't show every extreme that they name: `lengths`: in every draw some sequence has all 1536 slots filled.
All inputs are finite; a program needn't handle non-finite values.
Results may differ from a plain program's by a relative error of at most 0.0082.
Values may be sent and summed in bfloat16 or wider, within the bound.
A program may use at most 192 MiB of HBM per device.

v0:
```python
import math
import jax
import jax.numpy as jnp
from jax import lax
from jax.sharding import PartitionSpec as P

D = 9216


def attend_local(query, new_kv, cache, lengths):
    seqs = query.shape[0]
    head_dim = cache.shape[2] // 2
    heads = query.shape[1] // head_dim
    query_vectors = query.reshape(seqs, heads, head_dim)
    key_rows = cache[:, :, :head_dim]
    value_rows = cache[:, :, head_dim:]
    new_key = new_kv[:, :head_dim]
    new_value = new_kv[:, head_dim:]
    score_scale = 1.0 / math.sqrt(head_dim)
    attention_logits = (
        jnp.einsum("tgb,twb->tgw", query_vectors, key_rows, preferred_element_type=jnp.float32)
        * score_scale
    )
    own = (
        jnp.einsum("shd,sd->sh", query_vectors, new_key, preferred_element_type=jnp.float32)
        * score_scale
    )
    positions = lax.broadcasted_iota(jnp.int32, (1, 1, cache.shape[1]), 2)
    valid = positions < lengths[:, None, None]
    top = jnp.maximum(jnp.max(jnp.where(valid, attention_logits, own[:, :, None]), axis=2), own)
    weights = jnp.where(valid, jnp.exp(attention_logits - top[:, :, None]), jnp.float32(0.0))
    own_weight = jnp.exp(own - top)
    denom = jnp.sum(weights, axis=2) + own_weight
    attention_probabilities = (weights / denom[:, :, None]).astype(jnp.bfloat16)
    own_prob = (own_weight / denom).astype(jnp.bfloat16)
    value_mixture = jnp.einsum(
        "aqc,acn->aqn", attention_probabilities, value_rows, preferred_element_type=jnp.float32
    )
    value_mixture = (
        value_mixture
        + own_prob.astype(jnp.float32)[:, :, None] * new_value.astype(jnp.float32)[:, None, :]
    )
    return value_mixture.astype(jnp.bfloat16).reshape(seqs, heads * head_dim)


def body(
    stream,
    ln_gain,
    q_weight,
    kv_weight,
    out_weight,
    gate_weight,
    up_weight,
    down_weight,
    cache,
    lengths,
):
    values_f = stream.astype(jnp.float32)
    total, squares = lax.psum(
        (jnp.sum(values_f, axis=1), jnp.sum(values_f * values_f, axis=1)), "gx"
    )
    mean = total / D
    variance = squares / D - mean * mean
    normed = (
        (values_f - mean[:, None])
        * lax.rsqrt(variance + 1e-05)[:, None]
        * ln_gain.astype(jnp.float32)[None, :]
    ).astype(jnp.bfloat16)
    gathered = lax.all_gather(normed, "yz", axis=0, tiled=True)
    query_part = jnp.dot(gathered, q_weight, preferred_element_type=jnp.float32)
    kv_part = jnp.dot(gathered, kv_weight, preferred_element_type=jnp.float32)
    query_block, kv_block = (
        lax.psum_scatter(query_part, "gx", scatter_dimension=0, tiled=True),
        lax.psum_scatter(kv_part, "gx", scatter_dimension=0, tiled=True),
    )
    query_own, kv_own = (
        lax.all_to_all(
            query_block.astype(jnp.bfloat16), "yz", split_axis=0, concat_axis=1, tiled=True
        ),
        lax.all_to_all(
            kv_block.astype(jnp.bfloat16), "yz", split_axis=0, concat_axis=1, tiled=True
        ),
    )
    attended = attend_local(query_own, kv_own, cache, lengths)
    head_block = lax.all_to_all(attended, "yz", split_axis=1, concat_axis=0, tiled=True)
    head_all = lax.all_gather(head_block, "gx", axis=0, tiled=True)
    gate_part = jnp.dot(gathered, gate_weight, preferred_element_type=jnp.float32)
    up_part = jnp.dot(gathered, up_weight, preferred_element_type=jnp.float32)
    gate_share, up_share = (
        lax.psum_scatter(gate_part, "gx", scatter_dimension=0, tiled=True),
        lax.psum_scatter(up_part, "gx", scatter_dimension=0, tiled=True),
    )
    hidden_share = (jax.nn.silu(gate_share) * up_share).astype(jnp.bfloat16)
    hidden = lax.all_gather(hidden_share, "gx", axis=0, tiled=True)
    first = jnp.dot(head_all, out_weight, preferred_element_type=jnp.float32)
    update = lax.psum_scatter(
        first + jnp.dot(hidden, down_weight, preferred_element_type=jnp.float32),
        "yz",
        scatter_dimension=0,
        tiled=True,
    )
    return update.astype(jnp.bfloat16)


def solution(mesh):
    return jax.shard_map(
        body,
        mesh=mesh,
        in_specs=(
            P("yz", "gx"),
            P("gx"),
            P("gx", "yz"),
            P("gx", "yz"),
            P("yz", "gx"),
            P("gx", "yz"),
            P("gx", "yz"),
            P("yz", "gx"),
            P(("gx", "yz"), None, None),
            P(("gx", "yz")),
        ),
        out_specs=P("yz", "gx"),
        check_vma=False,
    )
```

profile of v0, /device:TPU:0, one launch (start us, length us, event | category | flops | bytes accessed | tf_op | source)
XLA Modules:
  0.0 278.6 jit_solution(908472190213945265)
XLA Ops:
  6.5 1.1 convert_reduce_fusion
  8.3 8.3 %all-reduce = (f32[16]{0:T(128)S(1)}, f32[16]{0:T(128)S(1)}) all-reduce(f32[16]{0:T(128)S(1)} %get-tuple-element.6, f32[16]{0:T(128)S(1)} %get-tuple-element.5), channel_id=1, replica_groups=mesh['gx'=4,'yz'=8] {'gx'}, use_global_device_ids=true, to_apply=%region_3.0 | all-reduce | flops 32 | bytes 256 | tf_op jit(solution)/shard_map/psum | solution.py:59
  16.6 1.0 fusion.20
  17.6 32.0 %all_gather.9 = bf16[128,2304]{1,0:T(8,128)(2,1)S(1)} all-gather(bf16[16,2304]{1,0:T(8,128)(2,1)S(1)} %fusion.20), channel_id=1, replica_groups=mesh['gx'=4,'yz'=8] {'yz'}, dimensions={0}, use_global_device_ids=true | all-gather | bytes 663552 | tf_op jit(solution)/shard_map/all_gather | solution.py:69
  50.6 5.0 %fusion.28 = f32[128,1536]{1,0:T(8,128)} fusion(bf16[128,2304]{1,0:T(8,128)(2,1)S(1)} %all_gather.9, bf16[2304,1536]{1,0:T(8,128)(2,1)} %param.12), kind=kOutput, calls=%fused_computation.38 | convolution fusion | flops 905969664 | bytes 8454144 | tf_op jit(solution)/shard_map/dot_general | solution.py:70
  55.6 11.4 %fusion.31 = f32[128,4608]{1,0:T(8,128)} fusion(bf16[128,2304]{1,0:T(8,128)(2,1)S(1)} %all_gather.9, bf16[2304,4608]{1,0:T(8,128)(2,1)} %param.16), kind=kOutput, calls=%fused_computation.41 | convolution fusion | flops 2717908992 | bytes 24182784 | tf_op jit(solution)/shard_map/dot_general | solution.py:88
  67.2 11.4 %fusion.30 = f32[128,4608]{1,0:T(8,128)} fusion(bf16[128,2304]{1,0:T(8,128)(2,1)S(1)} %all_gather.9, bf16[2304,4608]{1,0:T(8,128)(2,1)} %param.15), kind=kOutput, calls=%fused_computation.40 | convolution fusion | flops 2717908992 | bytes 24182784 | tf_op jit(solution)/shard_map/dot_general | solution.py:87
  80.0 5.4 %all-to-all-start.1 = ((bf16[8,2,128]{2,1,0:T(2,128)(2,1)}), bf16[8,2,128]{2,1,0:T(2,128)(2,1)S(1)}, u32[]{:S(2)}, u32[]{:S(2)}) async-start(bf16[8,2,128]{2,1,0:T(2,128)(2,1)} %reshape.47), calls=%async_computation.3 | async-start | bytes 8192 | tf_op jit(solution)/shard_map/all_to_all | solution.py:80
  85.4 6.3 %all-to-all-done.1 = bf16[8,2,128]{2,1,0:T(2,128)(2,1)S(1)} async-done(((bf16[8,2,128]{2,1,0:T(2,128)(2,1)}), bf16[8,2,128]{2,1,0:T(2,128)(2,1)S(1)}, u32[]{:S(2)}, u32[]{:S(2)}) %all-to-all-start.1) | async-done | bytes 4128 | tf_op jit(solution)/shard_map/all_to_all | solution.py:80
  91.9 4.2 %reduce-scatter.6.cloned.1.call-done = f32[32,1536]{1,0:T(8,128)} async-done(((f32[128,1536]{1,0:T(8,128)}), f32[32,1536]{1,0:T(8,128)}) %reduce-scatter.6.cloned.1.call-update) | async-done | bytes 196624 | tf_op jit(solution)/shard_map/reduce_scatter | solution.py:73
  96.1 0.9 convert_element_type.39
  97.7 5.5 %all-to-all-start = ((bf16[8,4,1536]{2,1,0:T(4,128)(2,1)}), bf16[8,4,1536]{2,1,0:T(4,128)(2,1)S(1)}, u32[]{:S(2)}, u32[]{:S(2)}) async-start(bf16[8,4,1536]{2,1,0:T(4,128)(2,1)} %all_to_all.40), calls=%async_computation.1 | async-start | bytes 196608 | tf_op jit(solution)/shard_map/all_to_all | solution.py:77
  103.3 7.1 %all-to-all-done = bf16[8,4,1536]{2,1,0:T(4,128)(2,1)S(1)} async-done(((bf16[8,4,1536]{2,1,0:T(4,128)(2,1)}), bf16[8,4,1536]{2,1,0:T(4,128)(2,1)S(1)}, u32[]{:S(2)}, u32[]{:S(2)}) %all-to-all-start) | async-done | bytes 98336 | tf_op jit(solution)/shard_map/all_to_all | solution.py:77
  110.6 21.2 %reduce-scatter.12.cloned.1.call-done = f32[32,4608]{1,0:T(8,128)} async-done(((f32[128,4608]{1,0:T(8,128)}), f32[32,4608]{1,0:T(8,128)}) %reduce-scatter.12.cloned.1.call-update) | async-done | bytes 589840 | tf_op jit(solution)/shard_map/reduce_scatter | solution.py:91
  131.8 35.7 %reduce-scatter.10.cloned.1.call-done = f32[32,4608]{1,0:T(8,128)} async-done(((f32[128,4608]{1,0:T(8,128)}), f32[32,4608]{1,0:T(8,128)}) %reduce-scatter.10.cloned.1.call-update) | async-done | bytes 589840 | tf_op jit(solution)/shard_map/reduce_scatter | solution.py:90
  167.5 2.1 multiply_convert_fusion
  169.7 3.0 %select_reduce_fusion = (f32[4,48]{1,0:T(4,128)S(1)}, f32[4,48,1536]{2,1,0:T(8,128)S(1)}) fusion(f32[4,48]{1,0:T(4,128)S(1)} %broadcast_multiply_fusion, pred[4,1536]{1,0:T(4,128)(4,1)S(1)} %iota_compare_fusion, bf16[4,48,256]{2,1,0:T(8,128)(2,1)S(1)} %reshape.44, bf16[4,1536,512]{2,1,0:T(8,128)(2,1)} %param.18), kind=kOutput, calls=%fused_computation.8 | convolution fusion | flops 151879488 | bytes 4431360 | tf_op jit(solution)/shard_map/tgb,twb->tgw/dot_general | solution.py:21
  173.1 2.6 fusion.10
  175.9 12.4 %all_to_all.54 = bf16[4,8,1536]{2,0,1:T(4,128)(2,1)S(1)} all-to-all(bf16[4,8,1536]{2,0,1:T(4,128)(2,1)S(1)} %copy.17), channel_id=1, replica_groups=mesh['gx'=4,'yz'=8] {'yz'}, dimensions={1} | all-to-all | bytes 196608 | tf_op jit(solution)/shard_map/all_to_all | solution.py:85
  188.4 6.3 %all_gather.10 = bf16[128,1536]{1,0:T(8,128)(2,1)S(1)} all-gather(bf16[32,1536]{1,0:T(8,128)(2,1)S(1)} %all_to_all.50), channel_id=1, replica_groups=mesh['gx'=4,'yz'=8] {'gx'}, dimensions={0}, use_global_device_ids=true | all-gather | bytes 491520 | tf_op jit(solution)/shard_map/all_gather | solution.py:86
  194.7 9.1 %fusion.32 = f32[128,2304]{1,0:T(8,128)S(1)} fusion(bf16[128,4608]{1,0:T(8,128)(2,1)} %all-gather.2.cloned.1.call-done, bf16[4608,2304]{1,0:T(8,128)(2,1)} %param.17), kind=kOutput, calls=%fused_computation.42 | convolution fusion | flops 2717908992 | bytes 23592960 | tf_op jit(solution)/shard_map/dot_general | solution.py:97
  203.8 5.2 %convolution_add_fusion = f32[128,2304]{1,0:T(8,128)} fusion(f32[128,2304]{1,0:T(8,128)S(1)} %fusion.32, bf16[128,1536]{1,0:T(8,128)(2,1)S(1)} %all_gather.10, bf16[1536,2304]{1,0:T(8,128)(2,1)} %param.14), kind=kOutput, calls=%fused_computation | convolution fusion | flops 906264576 | bytes 9830400 | tf_op jit(solution)/shard_map/dot_general | solution.py:95
  209.0 61.2 %reduce-scatter.14.cloned.1.call-done = f32[16,2304]{1,0:T(8,128)} async-done(((f32[128,2304]{1,0:T(8,128)}), f32[16,2304]{1,0:T(8,128)}) %reduce-scatter.14.cloned.1.call-update) | async-done | bytes 147472 | tf_op jit(solution)/shard_map/reduce_scatter | solution.py:96
  270.2 1.6 convert_element_type.47
  (41 shorter events, 5.1 us)
Async XLA Ops:
  6.5 43.0 %copy-start = (bf16[2304,64]{0,1:T(8,128)(2,1)S(1)}, bf16[2304,64]{0,1:T(8,128)(2,1)}, u32[]{:S(2)}) copy-start(bf16[2304,64]{0,1:T(8,128)(2,1)} %param.13) | copy-start | bytes 884740
  6.5 72.0 %reduce-scatter.8.cloned.1.call-start = ((), (), s32[]{:S(2)}) async-start(), calls=%async_computation.9 | async-start | bytes 81920 | tf_op jit(solution)/shard_map/reduce_scatter | solution.py:74
  50.5 45.6 %reduce-scatter.6.cloned.1.call-start = ((), (), s32[]{:S(2)}) async-start(), calls=%async_computation.8 | async-start | bytes 983040 | tf_op jit(solution)/shard_map/reduce_scatter | solution.py:73
  55.6 76.2 %reduce-scatter.12.cloned.1.call-start = ((), (), s32[]{:S(2)}) async-start(), calls=%async_computation.11 | async-start | bytes 2949120 | tf_op jit(solution)/shard_map/reduce_scatter | solution.py:91
  67.1 100.4 %reduce-scatter.10.cloned.1.call-start = ((), (), s32[]{:S(2)}) async-start(), calls=%async_computation.10 | async-start | bytes 2949120 | tf_op jit(solution)/shard_map/reduce_scatter | solution.py:90
  78.5 6.8 %copy-start.2 = (s32[4]{0:T(128)S(1)}, s32[4]{0:T(128)}, u32[]{:S(2)}) copy-start(s32[4]{0:T(128)} %param.19) | copy-start | bytes 52
  80.0 11.8 %all-to-all-start.1 = ((bf16[8,2,128]{2,1,0:T(2,128)(2,1)}), bf16[8,2,128]{2,1,0:T(2,128)(2,1)S(1)}, u32[]{:S(2)}, u32[]{:S(2)}) async-start(bf16[8,2,128]{2,1,0:T(2,128)(2,1)} %reshape.47), calls=%async_computation.3 | async-start | bytes 8192 | tf_op jit(solution)/shard_map/all_to_all | solution.py:80
  97.7 12.6 %all-to-all-start = ((bf16[8,4,1536]{2,1,0:T(4,128)(2,1)}), bf16[8,4,1536]{2,1,0:T(4,128)(2,1)S(1)}, u32[]{:S(2)}, u32[]{:S(2)}) async-start(bf16[8,4,1536]{2,1,0:T(4,128)(2,1)} %all_to_all.40), calls=%async_computation.1 | async-start | bytes 196608 | tf_op jit(solution)/shard_map/all_to_all | solution.py:77
  103.2 91.5 %all-gather.2.cloned.1.call-start = ((), (), s32[]{:S(2)}) async-start(), calls=%async_computation.12 | async-start | bytes 1474560 | tf_op jit(solution)/shard_map/all_gather | solution.py:94
  169.6 100.5 %reduce-scatter.14.cloned.1.call-start = ((), (), s32[]{:S(2)}) async-start(), calls=%async_computation.13 | async-start | bytes 1327104 | tf_op jit(solution)/shard_map/reduce_scatter | solution.py:96
  203.8 67.9 %copy-start.1 = (bf16[2304,64]{0,1:T(8,128)(2,1)S(1)}, bf16[2304,64]{0,1:T(8,128)(2,1)}, u32[]{:S(2)}) copy-start(bf16[2304,64]{0,1:T(8,128)(2,1)} %param.13) | copy-start | bytes 884740
Sparse Core Ops, SparseCore 0:
  50.6 19.4 reduce-scatter.7
  72.8 23.2 reduce-scatter.5
  98.7 33.1 reduce-scatter.11
  134.4 33.0 reduce-scatter.9
  169.8 17.4 all-gather.1
  209.1 61.0 reduce-scatter.13
where the time goes:
time: 279 us
  waiting for transfers between devices  136 us (49%)
  blocking collectives  59.1 us (21%)
  matrix products  48.8 us (17%)
  between operations  13.6 us (5%)
  starting transfers between devices  11.1 us (4%)
  other arithmetic  8.58 us (3%)
    reduce_scatter x1, waiting for transfers between devices, body(): lax.psum_scatter(first + jnp.dot(hidden, down_weight, preferred_element_t...  61.2 us
    reduce_scatter x1, waiting for transfers between devices, body(): lax.psum_scatter(gate_part, 'gx', scatter_dimension=0, tiled=True)  35.7 us
    all_gather x1, blocking collectives, body(): gathered = lax.all_gather(normed, 'yz', axis=0, tiled=True)  32 us
    reduce_scatter x1, waiting for transfers between devices, body(): lax.psum_scatter(up_part, 'gx', scatter_dimension=0, tiled=True)  21.2 us
    all_to_all x1, blocking collectives, body(): lax.all_to_all(attended, 'yz', split_axis=1, concat_axis=0, tiled=True)  12.4 us
    dot_general x1, matrix products, body(): up_part = jnp.dot(gathered, up_weight, preferred_element_type=jnp.float32)  11.4 us
    dot_general x1, matrix products, body(): jnp.dot(gathered, gate_weight, preferred_element_type=jnp.float32)  11.4 us
    dot_general x1, matrix products, body(): jnp.dot(hidden, down_weight, preferred_element_type=jnp.float32)  9.09 us
  transfers between devices with their start and end apart: 8, of which 6 were waited for; matrix products, arithmetic and copies ran while one was open for 13% of the time, Pallas kernels for 0%

commit v1 on v0

--- a/solution.py
+++ b/solution.py
@@ -5,6 +5,24 @@
 from jax.sharding import PartitionSpec as P
 
 D = 9216
+
+
+def laid_out(blocks, dim):
+    blocks = jnp.moveaxis(blocks, 0, dim)
+    lengths = blocks.shape
+    return blocks.reshape(*lengths[:dim], lengths[dim] * lengths[dim + 1], *lengths[dim + 2 :])
+
+
+def grow_blocks(x, axis):
+    size = lax.axis_size(axis)
+    blocks = x[None]
+    for level in range(size.bit_length() - 1):
+        stride = 1 << level
+        other = lax.ppermute(blocks, axis, [(i, i ^ stride) for i in range(size)])
+        both = jnp.stack([blocks, other])
+        upper = lax.axis_index(axis) >> level & 1
+        blocks = jnp.where(upper == 0, both, both[::-1]).reshape(-1, *x.shape)
+    return blocks
 
 
 def attend_local(query, new_kv, cache, lengths):
@@ -83,7 +101,7 @@
     )
     attended = attend_local(query_own, kv_own, cache, lengths)
     head_block = lax.all_to_all(attended, "yz", split_axis=1, concat_axis=0, tiled=True)
-    head_all = lax.all_gather(head_block, "gx", axis=0, tiled=True)
+    head_all = laid_out(grow_blocks(head_block, "gx"), 0)
     gate_part = jnp.dot(gathered, gate_weight, preferred_element_type=jnp.float32)
     up_part = jnp.dot(gathered, up_weight, preferred_element_type=jnp.float32)
     gate_share, up_share = (

time: 279 us -> 275 us (0.986)
  blocking collectives: 59.1 us -> 40.3 us
  waiting for transfers between devices: 136 us -> 145 us
  starting transfers between devices: 11.1 us -> 15.1 us
    all_to_all x1 -> x0, blocking collectives: 12.4 us -> none  [body(): lax.all_to_all(attended, 'yz', split_axis=1, concat_axis=0, tiled=True)]
    reduce_scatter x1, waiting for transfers between devices: 21.2 us -> 10.9 us  [body(): lax.psum_scatter(up_part, 'gx', scatter_dimension=0, tiled=True)]
    all_gather x1, waiting for transfers between devices: 0.01 us -> 8.77 us  [body(): hidden = lax.all_gather(hidden_share, 'gx', axis=0, tiled=True)]
    ppermute x0 -> x2, waiting for transfers between devices: none -> 7.89 us  [grow_blocks(): other = lax.ppermute(blocks, axis, [(i, i ^ stride) for i in range(size)])]
    all_gather x1 -> x0, blocking collectives: 6.33 us -> none  [body(): head_all = lax.all_gather(head_block, 'gx', axis=0, tiled=True)]
    all_to_all x0 -> x1, starting transfers between devices: none -> 3.36 us  [body(): lax.all_to_all(attended, 'yz', split_axis=1, concat_axis=0, tiled=True)]
    reduce_scatter x1, waiting for transfers between devices: 61.2 us -> 64.3 us  [body(): lax.psum_scatter(first + jnp.dot(hidden, down_weight, preferred_element_t...]
  transfers between devices with their start and end apart: 8 -> 11, of which waited for: 6 -> 9; matrix products, arithmetic and copies ran while one was open for 13% -> 14% of each run, Pallas kernels for 0% -> 0%
where the time goes in v1:
time: 275 us; the launch traced here: 274 us
  waiting for transfers between devices  145 us (53%)
  matrix products  48.8 us (18%)
  blocking collectives  40.3 us (15%)
  starting transfers between devices  15.1 us (5%)
  between operations  13.6 us (5%)
  other arithmetic  8.76 us (3%)
    reduce_scatter x1, waiting for transfers between devices, body(): lax.psum_scatter(first + jnp.dot(hidden, down_weight, preferred_element_t...  64.3 us
    reduce_scatter x1, waiting for transfers between devices, body(): lax.psum_scatter(gate_part, 'gx', scatter_dimension=0, tiled=True)  35.7 us
    all_gather x1, blocking collectives, body(): gathered = lax.all_gather(normed, 'yz', axis=0, tiled=True)  32 us
    dot_general x1, matrix products, body(): up_part = jnp.dot(gathered, up_weight, preferred_element_type=jnp.float32)  11.4 us
    dot_general x1, matrix products, body(): jnp.dot(gathered, gate_weight, preferred_element_type=jnp.float32)  11.4 us
    reduce_scatter x1, waiting for transfers between devices, body(): lax.psum_scatter(up_part, 'gx', scatter_dimension=0, tiled=True)  10.9 us
    dot_general x1, matrix products, body(): jnp.dot(hidden, down_weight, preferred_element_type=jnp.float32)  9.09 us
    all_gather x1, waiting for transfers between devices, body(): hidden = lax.all_gather(hidden_share, 'gx', axis=0, tiled=True)  8.77 us
  transfers between devices with their start and end apart: 11, of which 9 were waited for; matrix products, arithmetic and copies ran while one was open for 14% of the time, Pallas kernels for 0%

profile of v1, /device:TPU:0, one launch (start us, length us, event | category | flops | bytes accessed | tf_op | source)
XLA Modules:
  0.0 274.3 jit_solution(15994826065642661938)
XLA Ops:
  6.5 1.1 convert_reduce_fusion
  8.3 8.3 %all-reduce = (f32[16]{0:T(128)S(1)}, f32[16]{0:T(128)S(1)}) all-reduce(f32[16]{0:T(128)S(1)} %get-tuple-element.6, f32[16]{0:T(128)S(1)} %get-tuple-element.5), channel_id=1, replica_groups=mesh['gx'=4,'yz'=8] {'gx'}, use_global_device_ids=true, to_apply=%region_3.0 | all-reduce | flops 32 | bytes 256 | tf_op jit(solution)/shard_map/psum | solution.py:77
  17.6 32.0 %all_gather.6 = bf16[128,2304]{1,0:T(8,128)(2,1)S(1)} all-gather(bf16[16,2304]{1,0:T(8,128)(2,1)S(1)} %fusion.22), channel_id=1, replica_groups=mesh['gx'=4,'yz'=8] {'yz'}, dimensions={0}, use_global_device_ids=true | all-gather | bytes 663552 | tf_op jit(solution)/shard_map/all_gather | solution.py:87
  50.6 5.0 %fusion.30 = f32[128,1536]{1,0:T(8,128)} fusion(bf16[128,2304]{1,0:T(8,128)(2,1)S(1)} %all_gather.6, bf16[2304,1536]{1,0:T(8,128)(2,1)} %param.12), kind=kOutput, calls=%fused_computation.44 | convolution fusion | flops 905969664 | bytes 8454144 | tf_op jit(solution)/shard_map/dot_general | solution.py:88
  55.7 11.4 %fusion.33 = f32[128,4608]{1,0:T(8,128)} fusion(bf16[128,2304]{1,0:T(8,128)(2,1)S(1)} %all_gather.6, bf16[2304,4608]{1,0:T(8,128)(2,1)} %param.16), kind=kOutput, calls=%fused_computation.47 | convolution fusion | flops 2717908992 | bytes 24182784 | tf_op jit(solution)/shard_map/dot_general | solution.py:106
  67.2 11.4 %fusion.32 = f32[128,4608]{1,0:T(8,128)} fusion(bf16[128,2304]{1,0:T(8,128)(2,1)S(1)} %all_gather.6, bf16[2304,4608]{1,0:T(8,128)(2,1)} %param.15), kind=kOutput, calls=%fused_computation.46 | convolution fusion | flops 2717908992 | bytes 24182784 | tf_op jit(solution)/shard_map/dot_general | solution.py:105
  80.0 5.4 %all-to-all-start.1 = ((bf16[8,2,128]{2,1,0:T(2,128)(2,1)}), bf16[8,2,128]{2,1,0:T(2,128)(2,1)S(1)}, u32[]{:S(2)}, u32[]{:S(2)}) async-start(bf16[8,2,128]{2,1,0:T(2,128)(2,1)} %reshape.53), calls=%async_computation.3 | async-start | bytes 8192 | tf_op jit(solution)/shard_map/all_to_all | solution.py:98
  85.5 6.3 %all-to-all-done.1 = bf16[8,2,128]{2,1,0:T(2,128)(2,1)S(1)} async-done(((bf16[8,2,128]{2,1,0:T(2,128)(2,1)}), bf16[8,2,128]{2,1,0:T(2,128)(2,1)S(1)}, u32[]{:S(2)}, u32[]{:S(2)}) %all-to-all-start.1) | async-done | bytes 4128 | tf_op jit(solution)/shard_map/all_to_all | solution.py:98
  91.9 4.2 %reduce-scatter.6.cloned.1.call-done = f32[32,1536]{1,0:T(8,128)} async-done(((f32[128,1536]{1,0:T(8,128)}), f32[32,1536]{1,0:T(8,128)}) %reduce-scatter.6.cloned.1.call-update) | async-done | bytes 196624 | tf_op jit(solution)/shard_map/reduce_scatter | solution.py:91
  97.7 5.5 %all-to-all-start = ((bf16[8,4,1536]{2,1,0:T(4,128)(2,1)}), bf16[8,4,1536]{2,1,0:T(4,128)(2,1)S(1)}, u32[]{:S(2)}, u32[]{:S(2)}) async-start(bf16[8,4,1536]{2,1,0:T(4,128)(2,1)} %all_to_all.38), calls=%async_computation.1 | async-start | bytes 196608 | tf_op jit(solution)/shard_map/all_to_all | solution.py:95
  103.2 7.1 %all-to-all-done = bf16[8,4,1536]{2,1,0:T(4,128)(2,1)S(1)} async-done(((bf16[8,4,1536]{2,1,0:T(4,128)(2,1)}), bf16[8,4,1536]{2,1,0:T(4,128)(2,1)S(1)}, u32[]{:S(2)}, u32[]{:S(2)}) %all-to-all-start) | async-done | bytes 98336 | tf_op jit(solution)/shard_map/all_to_all | solution.py:95
  110.6 3.0 %select_reduce_fusion = (f32[4,48]{1,0:T(4,128)S(1)}, f32[4,48,1536]{2,1,0:T(8,128)S(1)}) fusion(f32[4,48]{1,0:T(4,128)S(1)} %broadcast_multiply_fusion, pred[4,1536]{1,0:T(4,128)(4,1)S(1)} %iota_compare_fusion, bf16[4,48,256]{2,1,0:T(8,128)(2,1)S(1)} %reshape.49, bf16[4,1536,512]{2,1,0:T(8,128)(2,1)} %param.18), kind=kOutput, calls=%fused_computation.8 | convolution fusion | flops 151879488 | bytes 4431360 | tf_op jit(solution)/shard_map/tgb,twb->tgw/dot_general | solution.py:39
  114.1 2.6 fusion.10
  117.5 3.4 %all-to-all-start.2 = ((bf16[4,8,1536]{2,0,1:T(4,128)(2,1)}), bf16[4,8,1536]{2,0,1:T(4,128)(2,1)S(1)}, u32[]{:S(2)}, u32[]{:S(2)}) async-start(bf16[4,8,1536]{2,0,1:T(4,128)(2,1)} %copy.17), calls=%async_computation.4 | async-start | bytes 196608 | tf_op jit(solution)/shard_map/all_to_all | solution.py:103
  120.9 10.9 %reduce-scatter.12.cloned.1.call-done = f32[32,4608]{1,0:T(8,128)} async-done(((f32[128,4608]{1,0:T(8,128)}), f32[32,4608]{1,0:T(8,128)}) %reduce-scatter.12.cloned.1.call-update) | async-done | bytes 589840 | tf_op jit(solution)/shard_map/reduce_scatter | solution.py:109
  131.8 35.7 %reduce-scatter.10.cloned.1.call-done = f32[32,4608]{1,0:T(8,128)} async-done(((f32[128,4608]{1,0:T(8,128)}), f32[32,4608]{1,0:T(8,128)}) %reduce-scatter.10.cloned.1.call-update) | async-done | bytes 589840 | tf_op jit(solution)/shard_map/reduce_scatter | solution.py:108
  167.5 2.1 multiply_convert_fusion
  170.1 1.2 collective-permute-done
  171.8 6.6 %collective-permute-done.1 = bf16[2,32,1536]{2,1,0:T(8,128)(2,1)S(1)} collective-permute-done((bf16[2,32,1536]{2,1,0:T(8,128)(2,1)S(1)}, bf16[2,32,1536]{2,1,0:T(8,128)(2,1)S(1)}, u32[]{:S(2)}, u32[]{:S(2)}) %collective-permute-start.1) | collective-permute-done | bytes 196640 | tf_op jit(solution)/shard_map/ppermute | solution.py:21
  178.5 8.8 %all-gather.2.cloned.1.call-done = bf16[128,4608]{1,0:T(8,128)(2,1)} async-done(((bf16[32,4608]{1,0:T(8,128)(2,1)}), bf16[128,4608]{1,0:T(8,128)(2,1)}) %all-gather.2.cloned.1.call-update) | async-done | bytes 1179664 | tf_op jit(solution)/shard_map/all_gather | solution.py:112
  187.3 9.1 %fusion.34 = f32[128,2304]{1,0:T(8,128)S(1)} fusion(bf16[128,4608]{1,0:T(8,128)(2,1)} %all-gather.2.cloned.1.call-done, bf16[4608,2304]{1,0:T(8,128)(2,1)} %param.17), kind=kOutput, calls=%fused_computation.48 | convolution fusion | flops 2717908992 | bytes 23592960 | tf_op jit(solution)/shard_map/dot_general | solution.py:115
  196.4 5.2 %convolution_add_fusion = f32[128,2304]{1,0:T(8,128)} fusion(f32[128,2304]{1,0:T(8,128)S(1)} %fusion.34, bf16[128,1536]{1,0:T(8,128)(2,1)S(1)} %bitcast.29, bf16[1536,2304]{1,0:T(8,128)(2,1)} %param.14), kind=kOutput, calls=%fused_computation | convolution fusion | flops 906264576 | bytes 9830400 | tf_op jit(solution)/shard_map/dot_general | solution.py:113
  201.6 64.3 %reduce-scatter.14.cloned.1.call-done = f32[16,2304]{1,0:T(8,128)} async-done(((f32[128,2304]{1,0:T(8,128)}), f32[16,2304]{1,0:T(8,128)}) %reduce-scatter.14.cloned.1.call-update) | async-done | bytes 147472 | tf_op jit(solution)/shard_map/reduce_scatter | solution.py:114
  265.9 1.6 convert_element_type.47
  (50 shorter events, 8.5 us)
Async XLA Ops:
  6.5 43.0 %copy-start = (bf16[2304,64]{0,1:T(8,128)(2,1)S(1)}, bf16[2304,64]{0,1:T(8,128)(2,1)}, u32[]{:S(2)}) copy-start(bf16[2304,64]{0,1:T(8,128)(2,1)} %param.13) | copy-start | bytes 884740
  6.5 72.1 %reduce-scatter.8.cloned.1.call-start = ((), (), s32[]{:S(2)}) async-start(), calls=%async_computation.9 | async-start | bytes 81920 | tf_op jit(solution)/shard_map/reduce_scatter | solution.py:92
  50.5 45.6 %reduce-scatter.6.cloned.1.call-start = ((), (), s32[]{:S(2)}) async-start(), calls=%async_computation.8 | async-start | bytes 983040 | tf_op jit(solution)/shard_map/reduce_scatter | solution.py:91
  55.6 76.2 %reduce-scatter.12.cloned.1.call-start = ((), (), s32[]{:S(2)}) async-start(), calls=%async_computation.11 | async-start | bytes 2949120 | tf_op jit(solution)/shard_map/reduce_scatter | solution.py:109
  67.1 100.4 %reduce-scatter.10.cloned.1.call-start = ((), (), s32[]{:S(2)}) async-start(), calls=%async_computation.10 | async-start | bytes 2949120 | tf_op jit(solution)/shard_map/reduce_scatter | solution.py:108
  78.6 6.8 %copy-start.2 = (s32[4]{0:T(128)S(1)}, s32[4]{0:T(128)}, u32[]{:S(2)}) copy-start(s32[4]{0:T(128)} %param.19) | copy-start | bytes 52
  80.0 11.8 %all-to-all-start.1 = ((bf16[8,2,128]{2,1,0:T(2,128)(2,1)}), bf16[8,2,128]{2,1,0:T(2,128)(2,1)S(1)}, u32[]{:S(2)}, u32[]{:S(2)}) async-start(bf16[8,2,128]{2,1,0:T(2,128)(2,1)} %reshape.53), calls=%async_computation.3 | async-start | bytes 8192 | tf_op jit(solution)/shard_map/all_to_all | solution.py:98
  97.7 12.6 %all-to-all-start = ((bf16[8,4,1536]{2,1,0:T(4,128)(2,1)}), bf16[8,4,1536]{2,1,0:T(4,128)(2,1)S(1)}, u32[]{:S(2)}, u32[]{:S(2)}) async-start(bf16[8,4,1536]{2,1,0:T(4,128)(2,1)} %all_to_all.38), calls=%async_computation.1 | async-start | bytes 196608 | tf_op jit(solution)/shard_map/all_to_all | solution.py:95
  117.5 52.4 %all-to-all-start.2 = ((bf16[4,8,1536]{2,0,1:T(4,128)(2,1)}), bf16[4,8,1536]{2,0,1:T(4,128)(2,1)S(1)}, u32[]{:S(2)}, u32[]{:S(2)}) async-start(bf16[4,8,1536]{2,0,1:T(4,128)(2,1)} %copy.17), calls=%async_computation.4 | async-start | bytes 196608 | tf_op jit(solution)/shard_map/all_to_all | solution.py:103
  120.9 66.4 %all-gather.2.cloned.1.call-start = ((), (), s32[]{:S(2)}) async-start(), calls=%async_computation.12 | async-start | bytes 1474560 | tf_op jit(solution)/shard_map/all_gather | solution.py:112
  169.7 96.3 %reduce-scatter.14.cloned.1.call-start = ((), (), s32[]{:S(2)}) async-start(), calls=%async_computation.13 | async-start | bytes 1327104 | tf_op jit(solution)/shard_map/reduce_scatter | solution.py:114
  169.9 1.4 collective-permute-start
  171.4 7.0 %collective-permute-start.1 = (bf16[2,32,1536]{2,1,0:T(8,128)(2,1)S(1)}, bf16[2,32,1536]{2,1,0:T(8,128)(2,1)S(1)}, u32[]{:S(2)}, u32[]{:S(2)}) collective-permute-start(bf16[2,32,1536]{2,1,0:T(8,128)(2,1)S(1)} %get-tuple-element.10), channel_id=1, source_target_pairs={{0,16},{8,24},{16,0},{24,8},{1,17},{9,25},{17,1},{25,9},{2,18},{10... | collective-permute-start | bytes 589832 | tf_op jit(solution)/shard_map/ppermute | solution.py:21
  196.4 71.1 %copy-start.1 = (bf16[2304,64]{0,1:T(8,128)(2,1)S(1)}, bf16[2304,64]{0,1:T(8,128)(2,1)}, u32[]{:S(2)}) copy-start(bf16[2304,64]{0,1:T(8,128)(2,1)} %param.13) | copy-start | bytes 884740
Sparse Core Ops, SparseCore 0:
  50.6 19.4 reduce-scatter.7
  72.8 23.2 reduce-scatter.5
  98.7 33.1 reduce-scatter.11
  134.4 33.0 reduce-scatter.9
  169.8 17.4 all-gather.1
  201.7 64.1 reduce-scatter.13
